TPU v7x, 1024 devices: a whole 4x8x16 slice. The times are simulated.
1024 devices in a mesh: dp: 8 (over y), lat: 16 (over z_lo, core), lon: 8 (over z_hi, x).
Axes of the slice: x: 4, y: 8, z: 16 (z_hi: 2, z_lo: 8; z = z_hi * 8 + z_lo), core: 2. Of those that a mesh axis runs over, the one named last changes fastest.
Arguments:
- field: bfloat16 [8, 128, 512, 384], P('dp', 'lat', 'lon'), may hold values from -6 to 6
- cotangent: bfloat16 [8, 128, 512, 384], P('dp', 'lat', 'lon'), may hold values from -6 to 6
- spectral_weight: bfloat16 [512, 128, 2, 512], P('dp', ('lat', 'lon')), may hold values from -0.1875 to 0.1875
Outputs:
- grad_input: bfloat16 [8, 128, 512, 384], P('dp', 'lat', 'lon')
- grad_weight: bfloat16 [512, 128, 2, 512], P('dp', ('lat', 'lon'))
All inputs are finite; a program needn't handle non-finite values.
Results may differ from a plain program's by a relative error of at most 0.019.
Values may be sent and summed in bfloat16 or wider, within the bound.
A program may use at most 32 MiB of HBM per device.

v0:
```python
import math

import jax
import jax.numpy as jnp
from jax import lax
from jax.sharding import PartitionSpec as P

M_DEV = 4


def in_blocks(value, dim, length):
    before, after = (value.shape[:dim], value.shape[dim + 1 :])
    return jnp.moveaxis(value.reshape(*before, length, -1, *after), dim, 0)


def joined_along(parts, dim):
    parts = jnp.moveaxis(parts, 0, dim)
    shape = parts.shape
    return parts.reshape(*shape[:dim], shape[dim] * shape[dim + 1], *shape[dim + 2 :])


def exchange_both(value, axis, axes, splits, concats):
    sizes = [lax.axis_size(a) for a in axes]
    parts = in_blocks(value, splits[0], sizes[0])
    parts = jnp.moveaxis(in_blocks(parts, splits[1] + 1, sizes[1]), 0, 1)
    inside = parts.shape[2:]
    parts = parts.reshape(-1, *inside)
    parts = lax.all_to_all(parts, axis, split_axis=0, concat_axis=0, tiled=True)
    parts = joined_along(parts.reshape(*sizes, *inside), concats[0] + 1)
    return joined_along(parts, concats[1])


def in_one_piece(arrays, axis, dim, along):
    ends, at = ([], 0)
    for a in arrays[:-1]:
        at += a.shape[along]
        ends.append(at)
    both = jnp.concatenate(arrays, axis=along)
    return tuple(jnp.split(lax.all_gather(both, axis, axis=dim, tiled=True), ends, axis=along))


def fourier_tables(nlon, norders):
    cols = jnp.arange(nlon, dtype=jnp.int32)[:, None]
    rows = jnp.arange(norders, dtype=jnp.int32)[None, :]
    phase = (cols * rows % nlon).astype(jnp.float32) * (2.0 * math.pi / nlon)
    cosine = jnp.cos(phase)
    sine = jnp.sin(phase)
    doubled = jnp.where(rows == 0, 1.0, 2.0).astype(jnp.float32)
    forward = jnp.stack([cosine / nlon, -sine / nlon], axis=-1)
    inverse = jnp.stack([doubled * cosine, -doubled * sine], axis=-1)
    return (forward.astype(jnp.bfloat16), inverse.astype(jnp.bfloat16))


def quad_weights(nlat):
    theta = math.pi * (jnp.arange(nlat, dtype=jnp.float32) + 0.5) / nlat
    return math.pi * jnp.sin(theta) / nlat


def legendre_rows(orders, nlat, ndeg):
    theta = math.pi * (jnp.arange(nlat, dtype=jnp.float32) + 0.5) / nlat
    cosine = jnp.cos(theta)[None, :]
    sine = jnp.sin(theta)[None, :]
    order_f = orders.astype(jnp.float32)[:, None]
    log_start = (
        0.5 * math.log(0.5)
        + 0.5
        * (
            lax.lgamma(2.0 * order_f + 2.0)
            - order_f * math.log(4.0)
            - 2.0 * lax.lgamma(order_f + 1.0)
        )
        + order_f * jnp.log(sine)
    )
    start = jnp.exp(log_start)

    def advance(carry, degree):
        older, newer = carry
        deg = degree.astype(jnp.float32)
        scale_a = jnp.sqrt(
            jnp.maximum(4.0 * deg * deg - 1.0, 0.0)
            / jnp.maximum(deg * deg - order_f * order_f, 1.0)
        )
        scale_b = jnp.sqrt(
            jnp.maximum((deg - 1.0) ** 2 - order_f * order_f, 0.0)
            / jnp.maximum(4.0 * (deg - 1.0) ** 2 - 1.0, 1.0)
        )
        general = scale_a * (cosine * newer - scale_b * older)
        value = jnp.where(deg < order_f, 0.0, jnp.where(deg == order_f, start, general))
        return ((newer, value), value)

    zeros = jnp.zeros(start.shape, jnp.float32)
    _, table = lax.scan(advance, (zeros, zeros), jnp.arange(ndeg, dtype=jnp.int32), unroll=16)
    return jnp.transpose(table, (1, 0, 2))


def gelu_slope(values):
    return 0.5 * (1.0 + lax.erf(values * (1.0 / math.sqrt(2.0)))) + values * jnp.exp(
        -0.5 * values * values
    ) * (1.0 / math.sqrt(2.0 * math.pi))


def by_latitude(values):
    return lax.all_to_all(values, "lat", split_axis=0, concat_axis=0, tiled=True)


def by_degree(values):
    return exchange_both(values, ("lat", "lon"), ("lat", "lon"), (0, 4), (0, 4))


def body(field, cotangent, spectral_weight):
    lat_count = lax.axis_size("lat")
    lon_count = lax.axis_size("lon")
    dp_count = lax.axis_size("dp")
    grid = field[0]
    grad_out = cotangent[0]
    rows_dev, slab, nlon = grid.shape
    nlat = rows_dev * lat_count
    orders = M_DEV * lat_count
    deg_dev = nlat // (lat_count * lon_count)
    width = slab * lon_count
    forward_tab, inverse_tab = fourier_tables(nlon, orders)
    local_orders = lax.axis_index("lat") * M_DEV + jnp.arange(M_DEV, dtype=jnp.int32)
    legendre = legendre_rows(local_orders, nlat, nlat)
    layout = (M_DEV, lat_count, lon_count, deg_dev, lat_count, rows_dev)
    analysis_leg = (
        (legendre * quad_weights(nlat)[None, None, :]).astype(jnp.bfloat16).reshape(layout)
    )
    synthesis_leg = legendre.astype(jnp.bfloat16).reshape(layout)

    def analyse(values, fourier, table):
        spectrum = jnp.einsum(
            "tqn,nmc->mtcq", values, fourier, preferred_element_type=jnp.float32
        ).astype(jnp.bfloat16)
        spectrum = by_latitude(spectrum.reshape(lat_count, M_DEV, rows_dev, 2 * slab))
        spectrum = spectrum.reshape(lat_count, M_DEV, rows_dev, 2, slab)
        coeff = jnp.einsum(
            "ibtcq,bxyrit->xrbcyq", spectrum, table, preferred_element_type=jnp.float32
        ).astype(jnp.bfloat16)
        return by_degree(coeff).reshape(lat_count, deg_dev, M_DEV, 2, width)

    def synthesise(coeff, table, fourier):
        moved = by_degree(coeff.reshape(lat_count, deg_dev, M_DEV, 2, lon_count, slab))
        spectrum = jnp.einsum(
            "xrbcyq,bxyrit->ibtcq", moved, table, preferred_element_type=jnp.float32
        ).astype(jnp.bfloat16)
        spectrum = by_latitude(spectrum.reshape(lat_count, M_DEV, rows_dev, 2 * slab))
        spectrum = spectrum.reshape(orders, rows_dev, 2, slab)
        return jnp.einsum("mtcq,nmc->tqn", spectrum, fourier, preferred_element_type=jnp.float32)

    coeff = analyse(grid, forward_tab, analysis_leg)
    weights = lax.all_gather(spectral_weight, "dp", axis=0, tiled=True)
    product = jnp.einsum("arbce,erdo->arbcdo", coeff, weights, preferred_element_type=jnp.float32)
    mixed = jnp.stack(
        [
            product[:, :, :, 0, 0] - product[:, :, :, 1, 1],
            product[:, :, :, 0, 1] + product[:, :, :, 1, 0],
        ],
        axis=3,
    ).astype(jnp.bfloat16)
    filtered = synthesise(mixed, synthesis_leg, inverse_tab)
    filtered_grad = (grad_out.astype(jnp.float32) * gelu_slope(filtered)).astype(jnp.bfloat16)
    mixed_grad = analyse(filtered_grad, inverse_tab, synthesis_leg)
    share = width // dp_count
    own_start = lax.axis_index("dp") * share
    coeff_piece, grad_piece = in_one_piece((coeff[None], mixed_grad[None]), "dp", 0, 1)
    own_rows = lax.dynamic_slice_in_dim(coeff_piece, own_start, share, 5)
    turned = jnp.stack([-own_rows[:, :, :, :, 1], own_rows[:, :, :, :, 0]], axis=4)
    paired_rows = jnp.stack([own_rows, turned], axis=4)
    summed = jnp.einsum(
        "sarbdce,sarbco->erdo", paired_rows, grad_piece, preferred_element_type=jnp.float32
    )
    grad_weight = (summed * (1.0 / dp_count)).astype(jnp.bfloat16)
    back = jnp.einsum("arbco,erdo->arbcde", mixed_grad, weights, preferred_element_type=jnp.float32)
    coeff_grad = jnp.stack(
        [back[:, :, :, 0, 0] + back[:, :, :, 1, 1], back[:, :, :, 1, 0] - back[:, :, :, 0, 1]],
        axis=3,
    ).astype(jnp.bfloat16)
    branch = synthesise(coeff_grad, analysis_leg, forward_tab)
    grad_input = (grad_out.astype(jnp.float32) + branch).astype(jnp.bfloat16)[None]
    return (grad_input, grad_weight)


def solution(mesh):
    return jax.shard_map(
        body,
        mesh=mesh,
        in_specs=(
            P("dp", "lat", "lon", None),
            P("dp", "lat", "lon", None),
            P("dp", ("lat", "lon"), None, None),
        ),
        out_specs=(P("dp", "lat", "lon", None), P("dp", ("lat", "lon"), None, None)),
        check_vma=False,
    )
```

profile of v0, /device:TPU:1, one launch (start us, length us, event | category | flops | bytes accessed | tf_op | source)
XLA Modules:
  0.0 329.4 jit_solution(14464092359839713116)
XLA Ops:
  9.8 18.0 %all-to-all-start = ((bf16[16,4,8,128]{3,2,1,0:T(8,128)(2,1)}), bf16[16,4,8,128]{3,2,1,0:T(8,128)(2,1)}, u32[]{:S(2)}, u32[]{:S(2)}) async-start(bf16[16,4,8,128]{3,2,1,0:T(8,128)(2,1)} %reshape.1702), calls=%async_computation | async-start | bytes 262144 | tf_op jit(solution)/shard_map/all_to_all | solution.py:103
  28.7 104.6 %while.21 = (s32[]{:T(128)}, f32[4,128]{1,0:T(4,128)S(1)}, f32[4,128]{1,0:T(4,128)S(1)}, f32[8,16,4,128]{3,2,1,0:T(4,128)S(1)}, s32[8,16]{1,0:T(8,128)S(1)}, /*i...) while((s32[]{:T(128)}, f32[4,128]{1,0:T(4,128)S(1)}, ...), condition=%wide.region_1.2_spmd.clone.clone.clone.clone, body=%wide.region_0.1_spmd.clone.clone.clone.clone.sunk | while | flops 68338 | bytes 263208 | solution.py:92
  134.0 2.4 reshape.1700
  136.4 1.2 copy.58
  137.7 1.7 reshape.1703
  139.4 1.4 fusion.54
  141.4 30.9 %all_to_all.40 = bf16[128,2,256]{2,1,0:T(2,128)(2,1)S(1)} all-to-all(bf16[128,2,256]{2,1,0:T(2,128)(2,1)S(1)} %reshape.1758), channel_id=1, replica_groups=mesh['dp'=8,'lat'=16,'lon'=8] {'lat','lon'}, dimensions={0} | all-to-all | bytes 262144 | tf_op jit(solution)/shard_map/all_to_all | solution.py:28
  172.9 1.6 convolution_bitcast_fusion.6
  176.0 7.5 %all-to-all-start.2 = ((bf16[128,2,256]{2,1,0:T(2,128)(2,1)}), bf16[128,2,256]{2,1,0:T(2,128)(2,1)}, u32[]{:S(2)}, u32[]{:S(2)}) async-start(bf16[128,2,256]{2,1,0:T(2,128)(2,1)} %reshape.1760), calls=%async_computation.2 | async-start | bytes 262144 | tf_op jit(solution)/shard_map/all_to_all | solution.py:28
  183.5 3.4 %reshape.1701 = bf16[4,16,8,16,8]{4,3,2,1,0:T(8,128)(2,1)} reshape(bf16[4,128,128]{2,1,0:T(8,128)(2,1)S(1)} %bitcast.614) | data formatting | bytes 262144 | tf_op jit(solution)/shard_map/reshape.67
  186.9 3.1 copy.63
  190.1 9.3 %all-to-all-done.2 = bf16[128,2,256]{2,1,0:T(2,128)(2,1)} async-done(((bf16[128,2,256]{2,1,0:T(2,128)(2,1)}), bf16[128,2,256]{2,1,0:T(2,128)(2,1)}, u32[]{:S(2)}, u32[]{:S(2)}) %all-to-all-start.2) | async-done | bytes 131104 | tf_op jit(solution)/shard_map/all_to_all | solution.py:28
  199.4 1.8 reshape.1761
  201.2 1.4 fusion.53
  203.7 4.8 %all-to-all-start.3 = ((bf16[16,4,8,128]{3,2,1,0:T(8,128)(2,1)}), bf16[16,4,8,128]{3,2,1,0:T(8,128)(2,1)S(1)}, u32[]{:S(2)}, u32[]{:S(2)}) async-start(bf16[16,4,8,128]{3,2,1,0:T(8,128)(2,1)} %reshape.1713), calls=%async_computation.3 | async-start | bytes 262144 | tf_op jit(solution)/shard_map/all_to_all | solution.py:103
  209.3 11.2 %all-to-all-done.3 = bf16[16,4,8,128]{3,2,1,0:T(8,128)(2,1)S(1)} async-done(((bf16[16,4,8,128]{3,2,1,0:T(8,128)(2,1)}), bf16[16,4,8,128]{3,2,1,0:T(8,128)(2,1)S(1)}, u32[]{:S(2)}, u32[]{:S(2)}) %all-to-all-start.3) | async-done | bytes 131104 | tf_op jit(solution)/shard_map/all_to_all | solution.py:103
  220.7 1.7 fusion.50
  223.5 5.0 %all-to-all-start.4 = ((bf16[16,4,8,128]{3,2,1,0:T(8,128)(2,1)}), bf16[16,4,8,128]{3,2,1,0:T(8,128)(2,1)S(1)}, u32[]{:S(2)}, u32[]{:S(2)}) async-start(bf16[16,4,8,128]{3,2,1,0:T(8,128)(2,1)} %reshape.1715), calls=%async_computation.4 | async-start | bytes 262144 | tf_op jit(solution)/shard_map/all_to_all | solution.py:103
  228.5 3.0 copy.68
  231.4 9.0 %all-to-all-done.4 = bf16[16,4,8,128]{3,2,1,0:T(8,128)(2,1)S(1)} async-done(((bf16[16,4,8,128]{3,2,1,0:T(8,128)(2,1)}), bf16[16,4,8,128]{3,2,1,0:T(8,128)(2,1)S(1)}, u32[]{:S(2)}, u32[]{:S(2)}) %all-to-all-start.4) | async-done | bytes 131104 | tf_op jit(solution)/shard_map/all_to_all | solution.py:103
  240.6 1.7 fusion.52
  243.6 10.9 %all-to-all-start.5 = ((bf16[128,2,256]{2,1,0:T(2,128)(2,1)}), bf16[128,2,256]{2,1,0:T(2,128)(2,1)S(1)}, u32[]{:S(2)}, u32[]{:S(2)}) async-start(bf16[128,2,256]{2,1,0:T(2,128)(2,1)} %reshape.1762), calls=%async_computation.5 | async-start | bytes 262144 | tf_op jit(solution)/shard_map/all_to_all | solution.py:28
  254.7 15.6 %all-to-all-done.5 = bf16[128,2,256]{2,1,0:T(2,128)(2,1)S(1)} async-done(((bf16[128,2,256]{2,1,0:T(2,128)(2,1)}), bf16[128,2,256]{2,1,0:T(2,128)(2,1)S(1)}, u32[]{:S(2)}, u32[]{:S(2)}) %all-to-all-start.5) | async-done | bytes 131104 | tf_op jit(solution)/shard_map/all_to_all | solution.py:28
  271.8 1.7 convolution_bitcast_fusion.3
  275.1 7.9 %all-to-all-start.6 = ((bf16[128,2,256]{2,1,0:T(2,128)(2,1)}), bf16[128,2,256]{2,1,0:T(2,128)(2,1)}, u32[]{:S(2)}, u32[]{:S(2)}) async-start(bf16[128,2,256]{2,1,0:T(2,128)(2,1)} %reshape.1764), calls=%async_computation.6 | async-start | bytes 262144 | tf_op jit(solution)/shard_map/all_to_all | solution.py:28
  282.9 2.1 copy.72
  285.0 13.7 %all-to-all-done.6 = bf16[128,2,256]{2,1,0:T(2,128)(2,1)} async-done(((bf16[128,2,256]{2,1,0:T(2,128)(2,1)}), bf16[128,2,256]{2,1,0:T(2,128)(2,1)}, u32[]{:S(2)}, u32[]{:S(2)}) %all-to-all-start.6) | async-done | bytes 131104 | tf_op jit(solution)/shard_map/all_to_all | solution.py:28
  298.7 1.1 reshape.1765
  301.4 4.9 %all-to-all-start.7 = ((bf16[16,4,8,128]{3,2,1,0:T(8,128)(2,1)}), bf16[16,4,8,128]{3,2,1,0:T(8,128)(2,1)S(1)}, u32[]{:S(2)}, u32[]{:S(2)}) async-start(bf16[16,4,8,128]{3,2,1,0:T(8,128)(2,1)} %reshape.1725), calls=%async_computation.7 | async-start | bytes 262144 | tf_op jit(solution)/shard_map/all_to_all | solution.py:103
  306.3 12.0 %all-to-all-done.7 = bf16[16,4,8,128]{3,2,1,0:T(8,128)(2,1)S(1)} async-done(((bf16[16,4,8,128]{3,2,1,0:T(8,128)(2,1)}), bf16[16,4,8,128]{3,2,1,0:T(8,128)(2,1)S(1)}, u32[]{:S(2)}, u32[]{:S(2)}) %all-to-all-start.7) | async-done | bytes 131104 | tf_op jit(solution)/shard_map/all_to_all | solution.py:103
  318.5 1.0 fusion.48
  319.5 1.5 split.9
  (507 shorter events, 37.8 us)
Async XLA Ops:
  7.2 1.1 copy-start
  7.2 20.6 %copy-start.11 = (bf16[64,1,2,512]{3,2,1,0:T(2,128)(2,1)S(1)}, bf16[64,1,2,512]{3,2,1,0:T(2,128)(2,1)}, u32[]{:S(2)}) copy-start(bf16[64,1,2,512]{3,2,1,0:T(2,128)(2,1)} %param.7) | copy-start | bytes 393220
  7.6 0.6 copy-start.6
  7.6 1.0 copy-start.8
  9.8 127.9 %all-to-all-start = ((bf16[16,4,8,128]{3,2,1,0:T(8,128)(2,1)}), bf16[16,4,8,128]{3,2,1,0:T(8,128)(2,1)}, u32[]{:S(2)}, u32[]{:S(2)}) async-start(bf16[16,4,8,128]{3,2,1,0:T(8,128)(2,1)} %reshape.1702), calls=%async_computation | async-start | bytes 262144 | tf_op jit(solution)/shard_map/all_to_all | solution.py:103
  27.8 145.1 %all-gather.3.cloned.1.call-start = ((), (), s32[]{:S(2)}) async-start(), calls=%async_computation.8 | async-start | bytes 1179648 | tf_op jit(solution)/shard_map/all_gather | solution.py:151
  133.3 0.7 copy-start.3
  172.6 2.5 copy-start.1
  172.8 10.7 %copy-start.4 = (f32[8,16,4,128]{3,2,1,0:T(4,128)S(1)}, f32[8,16,4,128]{3,2,1,0:T(4,128)}, u32[]{:S(2)}) copy-start(f32[8,16,4,128]{3,2,1,0:T(4,128)} %copy-done.3) | copy-start | bytes 786436
  176.0 23.4 %all-to-all-start.2 = ((bf16[128,2,256]{2,1,0:T(2,128)(2,1)}), bf16[128,2,256]{2,1,0:T(2,128)(2,1)}, u32[]{:S(2)}, u32[]{:S(2)}) async-start(bf16[128,2,256]{2,1,0:T(2,128)(2,1)} %reshape.1760), calls=%async_computation.2 | async-start | bytes 262144 | tf_op jit(solution)/shard_map/all_to_all | solution.py:28
  203.7 16.8 %all-to-all-start.3 = ((bf16[16,4,8,128]{3,2,1,0:T(8,128)(2,1)}), bf16[16,4,8,128]{3,2,1,0:T(8,128)(2,1)S(1)}, u32[]{:S(2)}, u32[]{:S(2)}) async-start(bf16[16,4,8,128]{3,2,1,0:T(8,128)(2,1)} %reshape.1713), calls=%async_computation.3 | async-start | bytes 262144 | tf_op jit(solution)/shard_map/all_to_all | solution.py:103
  223.5 16.9 %all-to-all-start.4 = ((bf16[16,4,8,128]{3,2,1,0:T(8,128)(2,1)}), bf16[16,4,8,128]{3,2,1,0:T(8,128)(2,1)S(1)}, u32[]{:S(2)}, u32[]{:S(2)}) async-start(bf16[16,4,8,128]{3,2,1,0:T(8,128)(2,1)} %reshape.1715), calls=%async_computation.4 | async-start | bytes 262144 | tf_op jit(solution)/shard_map/all_to_all | solution.py:103
  231.4 23.1 %copy-start.2 = (bf16[16,8,1,1,4,2,1,64]{7,1,0,5,4,6,3,2:T(8,128)(2,1)S(1)}, bf16[16,8,1,1,4,2,1,64]{7,1,0,5,4,6,3,2:T(8,128)(2,1)}, u32[]{:S(2)}) copy-start(bf16[16,8,1,1,4,2,1,64]{7,1,0,5,4,6,3,2:T(8,128)(2,1)} %copy-done.1) | copy-start | bytes 393220
  243.6 26.8 %all-to-all-start.5 = ((bf16[128,2,256]{2,1,0:T(2,128)(2,1)}), bf16[128,2,256]{2,1,0:T(2,128)(2,1)S(1)}, u32[]{:S(2)}, u32[]{:S(2)}) async-start(bf16[128,2,256]{2,1,0:T(2,128)(2,1)} %reshape.1762), calls=%async_computation.5 | async-start | bytes 262144 | tf_op jit(solution)/shard_map/all_to_all | solution.py:28
  254.5 65.0 %all-gather.5.cloned.1.call-start = ((), (), s32[]{:S(2)}) async-start(), calls=%async_computation.9 | async-start | bytes 2359296 | tf_op jit(solution)/shard_map/all_gather | solution.py:39
  275.1 23.7 %all-to-all-start.6 = ((bf16[128,2,256]{2,1,0:T(2,128)(2,1)}), bf16[128,2,256]{2,1,0:T(2,128)(2,1)}, u32[]{:S(2)}, u32[]{:S(2)}) async-start(bf16[128,2,256]{2,1,0:T(2,128)(2,1)} %reshape.1764), calls=%async_computation.6 | async-start | bytes 262144 | tf_op jit(solution)/shard_map/all_to_all | solution.py:28
  285.0 33.5 %copy-start.7 = (bf16[384,64,1]{0,1,2:T(8,128)(2,1)S(1)}, bf16[384,64,1]{0,1,2:T(8,128)(2,1)}, u32[]{:S(2)}) copy-start(bf16[384,64,1]{0,1,2:T(8,128)(2,1)} %copy-done.6) | copy-start | bytes 147460
  285.0 33.5 %copy-start.9 = (bf16[384,64,1]{0,1,2:T(8,128)(2,1)S(1)}, bf16[384,64,1]{0,1,2:T(8,128)(2,1)}, u32[]{:S(2)}) copy-start(bf16[384,64,1]{0,1,2:T(8,128)(2,1)} %copy-done.8) | copy-start | bytes 147460
  285.0 33.5 %copy-start.10 = (bf16[1,8,64,384]{3,2,1,0:T(8,128)(2,1)S(1)}, bf16[1,8,64,384]{3,2,1,0:T(8,128)(2,1)}, u32[]{:S(2)}) copy-start(bf16[1,8,64,384]{3,2,1,0:T(8,128)(2,1)} %param.6) | copy-start | bytes 1179652
  301.4 16.9 %all-to-all-start.7 = ((bf16[16,4,8,128]{3,2,1,0:T(8,128)(2,1)}), bf16[16,4,8,128]{3,2,1,0:T(8,128)(2,1)S(1)}, u32[]{:S(2)}, u32[]{:S(2)}) async-start(bf16[16,4,8,128]{3,2,1,0:T(8,128)(2,1)} %reshape.1725), calls=%async_computation.7 | async-start | bytes 262144 | tf_op jit(solution)/shard_map/all_to_all | solution.py:103
  319.5 1.9 copy-start.5
Sparse Core Ops, SparseCore 0:
  31.8 40.5 all-gather.2
  271.7 36.4 all-gather.4
where the time goes:
time: 332 us; the launch traced here: 329 us
  loops' own time  84.4 us (25%)
  waiting for transfers between devices  70.9 us (21%)
  starting transfers between devices  59.1 us (18%)
  local copies, waits for them, and re-layouts  40.9 us (12%)
  blocking collectives  30.9 us (9%)
  other arithmetic  17 us (5%)
  between operations  14.6 us (4%)
  matrix products  11.7 us (4%)
    another operation x1, loops' own time, legendre_rows(): lax.scan(advance, (zeros, zeros), jnp.arange(ndeg, dtype=jnp.int32), unro...  84.4 us
    all_to_all x3, waiting for transfers between devices, exchange_both(): parts = lax.all_to_all(parts, axis, split_axis=0, concat_axis=0, tiled=True)  38.6 us
    all_to_all x4, starting transfers between devices, by_latitude(): lax.all_to_all(values, 'lat', split_axis=0, concat_axis=0, tiled=True)  32.7 us
    all_to_all x4, waiting for transfers between devices, by_latitude(): lax.all_to_all(values, 'lat', split_axis=0, concat_axis=0, tiled=True)  32.2 us
    all_to_all x1, blocking collectives, exchange_both(): parts = lax.all_to_all(parts, axis, split_axis=0, concat_axis=0, tiled=True)  30.9 us
    all_to_all x3, starting transfers between devices, exchange_both(): parts = lax.all_to_all(parts, axis, split_axis=0, concat_axis=0, tiled=True)  26.3 us
    another operation x8, local copies, waits for them, and re-layouts  15.6 us
    while x120, other arithmetic  10.1 us
  transfers between devices with their start and end apart: 9, of which 6 were waited for; matrix products, arithmetic and copies ran while one was open for 15% of the time, Pallas kernels for 0%

commit v1 on v0

v1 whole, which is shorter than its diff:
```python
import functools
import math

import jax
import jax.numpy as jnp
import numpy as np
from jax import lax
from jax.experimental import pallas as pl
from jax.experimental.pallas import tpu as pltpu
from jax.sharding import PartitionSpec as P

MESH = pl.DeviceIdType.MESH
BF16 = jnp.bfloat16
F32 = jnp.float32
M_DEV = 4
ROWS = 8
SLAB = 64
N_EXCHANGES = 8
SEM_WEIGHTS, SEM_COEFF, SEM_GRADS = 8, 9, 10


def fourier_tables(nlon, norders):
    cols = np.arange(nlon, dtype=np.int32)[None, :]
    rows = np.arange(norders, dtype=np.int32)[:, None]
    phase = (cols * rows % nlon).astype(np.float32) * np.float32(2.0 * math.pi / nlon)
    cosine, sine = np.cos(phase), np.sin(phase)
    doubled = np.where(rows == 0, 1.0, 2.0).astype(np.float32)
    forward = np.concatenate([cosine / np.float32(nlon), -sine / np.float32(nlon)])
    inverse = np.concatenate([doubled * cosine, -doubled * sine])
    return jnp.asarray(forward, BF16), jnp.asarray(inverse, BF16)


def legendre_seeds(nlat, norders):
    theta = np.float32(math.pi) * (np.arange(nlat, dtype=np.float32) + np.float32(0.5)) / np.float32(nlat)
    theta = theta.astype(np.float64)
    seeds = np.zeros((norders // M_DEV, 8, nlat), np.float32)
    for m in range(norders):
        scale = math.lgamma(2.0 * m + 2.0) - m * math.log(4.0) - 2.0 * math.lgamma(m + 1.0)
        start = 0.5 * math.log(0.5) + 0.5 * scale + m * np.log(np.sin(theta))
        seeds[m // M_DEV, m % M_DEV] = np.exp(start).astype(np.float32)
    rows = np.zeros((8, nlat), np.float32)
    rows[0] = np.cos(theta)
    rows[1] = math.pi * np.sin(theta) / nlat
    return jnp.asarray(seeds.reshape(-1, nlat)), jnp.asarray(rows)


def swap_halves(tile):
    return pltpu.roll(tile, 64, axis=1)


def low_lanes(shape):
    return lax.broadcasted_iota(jnp.int32, shape, 1) < 64


def gelu_slope(values):
    return 0.5 * (1.0 + lax.erf(values * (1.0 / math.sqrt(2.0)))) + values * jnp.exp(
        -0.5 * values * values
    ) * (1.0 / math.sqrt(2.0 * math.pi))


def kernel(
    sizes,
    x_ref,
    g_ref,
    w_ref,
    forward_ref,
    inverse_ref,
    seeds_ref,
    rows_ref,
    out_ref,
    gw_ref,
    by_lat_out,
    by_lat_in,
    by_deg_out,
    by_deg_in,
    wide,
    coeff_all,
    grads_all,
    mixing,
    hbuf,
    fgrad,
    stage,
    leg,
    analysis,
    analysis_t,
    synthesis,
    synthesis_t,
    send_sem,
    recv_sem,
):
    n_dp, n_lat, n_lon = sizes
    n_x = min(n_lon, 4)
    n_zlo = n_lat // 2
    n_z = n_zlo * (n_lon // n_x)
    orders = n_lat * M_DEV
    n_deg = n_lat * n_lon
    nlat = n_lat * ROWS
    mrows = orders
    s = lax.axis_index("dp")
    a = lax.axis_index("lat")
    y = lax.axis_index("lon")
    chip, core = lax.div(a, 2), lax.rem(a, 2)
    x, zhi = lax.rem(y, n_x), lax.div(y, n_x)
    z = zhi * n_zlo + chip

    def over_degree_group(visit):
        def step(k, carry):
            half = lax.div(k + 1, 2)
            off = jnp.where(lax.rem(k, 2) == 1, n_z // 2 - half, n_z // 2 + half)
            zt = lax.rem(z + off, n_z)
            zl, zh = lax.rem(zt, n_zlo), lax.div(zt, n_zlo)
            for dx in list(range(n_x // 2, 0, -1)) + list(range(n_x // 2 + 1, n_x)) + [0]:
                for dc in (1, 0):
                    la = zl * 2 + lax.rem(core + dc, 2)
                    lo = zh * n_x + lax.rem(x + dx, n_x)
                    if dx == 0 and dc == 0:
                        pl.when(k < n_z - 1)(functools.partial(visit, la, lo))
                    else:
                        visit(la, lo)
            return carry

        lax.fori_loop(0, n_z, step, 0)

    def over_lat_group(visit):
        for d in range(n_zlo - 1, 0, -1):
            for q in (chip + d, chip - d):

                @pl.when((q >= 0) & (q < n_zlo))
                def _(q=q):
                    visit(q * 2)
                    visit(q * 2 + 1)

        visit(chip * 2 + 1 - core)

    def over_dp_group(visit):
        for d in list(range(n_dp // 2, 0, -1)) + list(range(n_dp // 2 + 1, n_dp)):
            visit(lax.rem(s + d, n_dp))

    def remote(src, dst, sem, device):
        pltpu.make_async_remote_copy(
            src_ref=src,
            dst_ref=dst,
            send_sem=send_sem.at[sem],
            recv_sem=recv_sem.at[sem],
            device_id=device,
            device_id_type=MESH,
        ).start()

    def local(src, dst, sem):
        pltpu.make_async_copy(src, dst, recv_sem.at[sem]).start()

    def arrived(ref, sem):
        pltpu.make_async_copy(ref, ref, recv_sem.at[sem]).wait()

    def sent(ref, sem):
        pltpu.make_async_copy(ref, ref, send_sem.at[sem]).wait()

    def send_by_lat(e, k):
        src, dst = by_lat_out.at[k], by_lat_in.at[k]
        over_lat_group(lambda j: remote(src.at[j], dst.at[a], e, {"lat": j}))
        local(src.at[a], dst.at[a], e)

    def send_to_degrees(e, k):
        src, dst = by_deg_out.at[k], by_deg_in.at[k]
        mine = y * n_lat + a
        over_degree_group(
            lambda la, lo: remote(src.at[la * n_lon + lo], dst.at[mine], e, {"lat": la, "lon": lo})
        )
        local(src.at[a * n_lon + y], dst.at[mine], e)

    def send_to_orders(e, k):
        src, dst = by_deg_out.at[k], by_deg_in.at[k]
        mine = a * n_lon + y
        over_degree_group(
            lambda la, lo: remote(src.at[lo * n_lat + la], dst.at[mine], e, {"lat": la, "lon": lo})
        )
        local(src.at[y * n_lat + a], dst.at[mine], e)

    def to_spectrum(table, values, k):
        out = lax.dot_general(
            table, values, (((1,), (1,)), ((), ())), preferred_element_type=F32
        )
        low = low_lanes((orders, 128))
        for j in range(ROWS // 2):
            real = out[:orders, j * 128 : (j + 1) * 128]
            imag = out[orders:, j * 128 : (j + 1) * 128]
            stage[pl.ds(2 * j, orders, stride=ROWS), :] = jnp.where(low, real, swap_halves(imag))
            stage[pl.ds(2 * j + 1, orders, stride=ROWS), :] = jnp.where(low, swap_halves(real), imag)
        by_lat_out[k] = stage[: orders * ROWS, :].astype(BF16).reshape(n_lat, M_DEV * ROWS, 128)

    def to_degrees(tables, k_in, k):
        for m in range(M_DEV):
            part = by_lat_in[k_in, :, m * ROWS : (m + 1) * ROWS, :]
            part = part.astype(F32).reshape(nlat, 128).astype(BF16)
            stage[pl.ds(m, n_deg, stride=M_DEV), :] = jnp.dot(
                tables[m], part, preferred_element_type=F32
            )
        by_deg_out[k] = stage[: n_deg * M_DEV, :].reshape(n_deg, M_DEV, 128).astype(BF16)

    def gather_wide(k):
        for j in range(n_lon):
            part = by_deg_in[k, j * n_lat : (j + 1) * n_lat]
            wide[:, j * 128 : (j + 1) * 128] = part.astype(F32).reshape(mrows, 128).astype(BF16)

    def scatter_wide(value, k):
        for j in range(n_lon):
            part = value[:, j * 128 : (j + 1) * 128].reshape(n_lat, M_DEV, 128)
            by_deg_out[k, j * n_lat : (j + 1) * n_lat] = part.astype(BF16)

    def to_rows(tables, k_in, k):
        stage[: n_deg * M_DEV, :] = by_deg_in[k_in].astype(F32).reshape(n_deg * M_DEV, 128)
        parts = []
        for m in range(M_DEV):
            part = stage[pl.ds(m, n_deg, stride=M_DEV), :].astype(BF16)
            out = jnp.dot(tables[m], part, preferred_element_type=F32)
            parts.append(out.reshape(n_lat, ROWS, 128))
        both = jnp.stack(parts, axis=1).reshape(n_lat, M_DEV * ROWS, 128)
        by_lat_out[k] = both.astype(BF16)

    def to_grid(table_ref, k, use):
        stage[: orders * ROWS, :] = by_lat_in[k].astype(F32).reshape(orders * ROWS, 128)
        low = low_lanes((orders, 128))
        for j in range(ROWS // 2):
            even = stage[pl.ds(2 * j, orders, stride=ROWS), :]
            odd = stage[pl.ds(2 * j + 1, orders, stride=ROWS), :]
            real = jnp.where(low, even, swap_halves(odd))
            imag = jnp.where(low, swap_halves(even), odd)
            both = jnp.concatenate([real, imag], axis=0).astype(BF16)
            use(
                slice(j * 128, (j + 1) * 128),
                lax.dot_general(
                    both, table_ref[...], (((0,), (0,)), ((), ())), preferred_element_type=F32
                ),
            )

    barrier = pltpu.get_barrier_semaphore()

    def greet(device):
        pl.semaphore_signal(barrier, inc=1, device_id=device, device_id_type=MESH)

    over_degree_group(lambda la, lo: greet({"lat": la, "lon": lo}))
    over_dp_group(lambda j: greet({"dp": j}))

    to_spectrum(forward_ref[...], x_ref[...], 0)
    pl.semaphore_wait(barrier, n_deg - 1 + n_dp - 1)

    send_by_lat(0, 0)
    own_rows = pl.ds(pl.multiple_of(s * 128, 128), 64)
    over_dp_group(lambda j: remote(w_ref, mixing.at[own_rows, :], SEM_WEIGHTS, {"dp": j}))
    local(w_ref, mixing.at[own_rows, :], SEM_WEIGHTS)

    order = (a * M_DEV + lax.broadcasted_iota(jnp.int32, (8, nlat), 0)).astype(F32)
    order_sq = order * order
    cosine = jnp.broadcast_to(rows_ref[0:1, :], (8, nlat))
    start = seeds_ref[pl.ds(pl.multiple_of(a * 8, 8), 8), :]

    def advance(degree, carry):
        older, newer, deg = carry
        below = deg - 1.0
        scale_a = jnp.sqrt(
            jnp.maximum(4.0 * deg * deg - 1.0, 0.0) / jnp.maximum(deg * deg - order_sq, 1.0)
        )
        scale_b = jnp.sqrt(
            jnp.maximum(below * below - order_sq, 0.0)
            / jnp.maximum(4.0 * (below * below) - 1.0, 1.0)
        )
        general = scale_a * (cosine * newer - scale_b * older)
        value = jnp.where(deg < order, 0.0, jnp.where(deg == order, start, general))
        leg[pl.ds(pl.multiple_of(degree * 8, 8), 8), :] = value
        return newer, value, deg + 1.0

    zeros = start * 0.0
    lax.fori_loop(0, n_deg, advance, (zeros, zeros, zeros), unroll=8)
    for m in range(M_DEV):
        table = leg[pl.ds(m, n_deg, stride=8), :]
        weighted = table * rows_ref[1:2, :]
        synthesis[m] = table.astype(BF16)
        analysis[m] = weighted.astype(BF16)
        synthesis_t[m] = table.T.astype(BF16)
        analysis_t[m] = weighted.T.astype(BF16)

    arrived(by_lat_in.at[0], 0)
    to_degrees(analysis, 0, 0)
    send_to_degrees(1, 0)

    arrived(wide_shape(mixing, n_lon), SEM_WEIGHTS)
    low = low_lanes((64, 128))
    for j in range(n_lon):
        for i in range(n_lon):
            turned = swap_halves(mixing[j * 128 : j * 128 + 64, i * 128 : (i + 1) * 128].astype(F32))
            mixing[j * 128 + 64 : (j + 1) * 128, i * 128 : (i + 1) * 128] = jnp.where(
                low, -turned, turned
            ).astype(BF16)

    arrived(by_deg_in.at[0], 1)
    gather_wide(0)
    scatter_wide(jnp.dot(wide[...], mixing[...], preferred_element_type=F32), 1)
    send_to_orders(2, 1)

    def coeff_block(j):
        return by_deg_in.at[0, pl.ds(j * n_lat, n_lat)]

    over_dp_group(lambda j: remote(coeff_block(j), coeff_all.at[s], SEM_COEFF, {"dp": j}))
    local(coeff_block(s), coeff_all.at[s], SEM_COEFF)

    arrived(by_deg_in.at[1], 2)
    to_rows(synthesis_t, 1, 1)
    send_by_lat(3, 1)
    arrived(by_lat_in.at[1], 3)

    def slope(rows, filtered):
        fgrad[rows, :] = (g_ref[rows, :].astype(F32) * gelu_slope(filtered)).astype(BF16)

    to_grid(inverse_ref, 1, slope)
    to_spectrum(inverse_ref[...], fgrad[...], 2)
    send_by_lat(4, 2)
    arrived(by_lat_in.at[2], 4)
    to_degrees(synthesis, 2, 2)
    send_to_degrees(5, 2)
    arrived(by_deg_in.at[2], 5)

    gather_wide(2)
    over_dp_group(lambda j: remote(by_deg_in.at[2], grads_all.at[s], SEM_GRADS, {"dp": j}))
    local(by_deg_in.at[2], grads_all.at[s], SEM_GRADS)
    scatter_wide(
        lax.dot_general(
            wide[...], mixing[...], (((1,), (1,)), ((), ())), preferred_element_type=F32
        ),
        3,
    )
    send_to_orders(6, 3)
    arrived(by_deg_in.at[3], 6)
    to_rows(analysis_t, 3, 3)
    send_by_lat(7, 3)
    arrived(by_lat_in.at[3], 7)

    def finish(rows, branch):
        out_ref[rows, :] = (g_ref[rows, :].astype(F32) + branch).astype(BF16)

    to_grid(forward_ref, 3, finish)

    arrived(coeff_all, SEM_COEFF)
    arrived(grads_all, SEM_GRADS)
    for i in range(n_dp):
        for j in range(n_lon):
            part = grads_all[i, j * n_lat : (j + 1) * n_lat]
            hbuf[i * mrows : (i + 1) * mrows, j * 128 : (j + 1) * 128] = (
                part.astype(F32).reshape(mrows, 128).astype(BF16)
            )
    parts = coeff_all[...].astype(F32).reshape(n_dp * mrows, 128).astype(BF16)
    total = lax.dot_general(
        parts, hbuf[...], (((0,), (0,)), ((), ())), preferred_element_type=F32
    )
    for j in range(n_lon):
        real = total[:64, j * 128 : (j + 1) * 128]
        imag = swap_halves(total[64:, j * 128 : (j + 1) * 128])
        gw_ref[:, j * 128 : (j + 1) * 128] = (
            jnp.where(low, real + imag, real - imag) * (1.0 / n_dp)
        ).astype(BF16)

    for e, k in ((0, 0), (3, 1), (4, 2), (7, 3)):
        sent(by_lat_out.at[k, pl.ds(0, n_lat - 1)], e)
    for e, k in ((1, 0), (2, 1), (5, 2), (6, 3)):
        sent(by_deg_out.at[k, pl.ds(0, n_deg - 1)], e)
    sent(coeff_all.at[pl.ds(0, n_dp - 1)], SEM_COEFF)
    sent(grads_all.at[pl.ds(0, n_dp - 1)], SEM_GRADS)
    sent(mixing.at[pl.ds(0, 64 * (n_dp - 1)), :], SEM_WEIGHTS)


def wide_shape(mixing, n_lon):
    return mixing.at[pl.ds(0, 64 * n_lon), :]


def body(sizes, field, cotangent, spectral_weight):
    n_dp, n_lat, n_lon = sizes
    nlon = field.shape[3]
    orders, n_deg, nlat = n_lat * M_DEV, n_lat * n_lon, n_lat * ROWS
    width = n_lon * 128
    rows = ROWS * SLAB
    forward, inverse = fourier_tables(nlon, orders)
    seeds, lat_rows = legendre_seeds(nlat, orders)
    weights = spectral_weight.reshape(64, 2, n_lon, 64).transpose(0, 2, 1, 3).reshape(64, width)
    vmem = pl.BlockSpec(memory_space=pltpu.VMEM)
    grad_input, grad_weight = pl.pallas_call(
        functools.partial(kernel, sizes),
        out_shape=(
            jax.ShapeDtypeStruct((rows, nlon), BF16),
            jax.ShapeDtypeStruct((64, width), BF16),
        ),
        in_specs=[vmem] * 7,
        out_specs=(vmem, vmem),
        scratch_shapes=[
            pltpu.VMEM((4, n_lat, M_DEV * ROWS, 128), BF16),
            pltpu.VMEM((4, n_lat, M_DEV * ROWS, 128), BF16),
            pltpu.VMEM((4, n_deg, M_DEV, 128), BF16),
            pltpu.VMEM((4, n_deg, M_DEV, 128), BF16),
            pltpu.VMEM((orders, width), BF16),
            pltpu.VMEM((n_dp, n_lat, M_DEV, 128), BF16),
            pltpu.VMEM((n_dp, n_deg, M_DEV, 128), BF16),
            pltpu.VMEM((width, width), BF16),
            pltpu.VMEM((n_dp * orders, width), BF16),
            pltpu.VMEM((rows, nlon), BF16),
            pltpu.VMEM((max(n_deg * M_DEV, orders * ROWS), 128), F32),
            pltpu.VMEM((n_deg * 8, nlat), F32),
            pltpu.VMEM((M_DEV, n_deg, nlat), BF16),
            pltpu.VMEM((M_DEV, nlat, n_deg), BF16),
            pltpu.VMEM((M_DEV, n_deg, nlat), BF16),
            pltpu.VMEM((M_DEV, nlat, n_deg), BF16),
            pltpu.SemaphoreType.DMA((11,)),
            pltpu.SemaphoreType.DMA((11,)),
        ],
        compiler_params=pltpu.CompilerParams(
            collective_id=0, has_side_effects=True, vmem_limit_bytes=48 * 1024 * 1024
        ),
        name="block",
    )(
        field.reshape(rows, nlon),
        cotangent.reshape(rows, nlon),
        weights,
        forward,
        inverse,
        seeds,
        lat_rows,
    )
    grad_weight = grad_weight.reshape(64, n_lon, 2, 64).transpose(0, 2, 1, 3)
    return (
        grad_input.reshape(1, ROWS, SLAB, nlon),
        grad_weight.reshape(64, 1, 2, n_lon * SLAB),
    )


def solution(mesh):
    sizes = (mesh.shape["dp"], mesh.shape["lat"], mesh.shape["lon"])
    return jax.shard_map(
        functools.partial(body, sizes),
        mesh=mesh,
        in_specs=(
            P("dp", "lat", "lon", None),
            P("dp", "lat", "lon", None),
            P("dp", ("lat", "lon"), None, None),
        ),
        out_specs=(P("dp", "lat", "lon", None), P("dp", ("lat", "lon"), None, None)),
        check_vma=False,
    )
```

time: 332 us -> 119 us (0.36)
  Pallas kernels: 0 us -> 114 us
  loops' own time: 84.4 us -> 0 us
  waiting for transfers between devices: 70.9 us -> 0 us
  starting transfers between devices: 59.1 us -> 0 us
  local copies, waits for them, and re-layouts: 40.9 us -> 4.12 us
  blocking collectives: 30.9 us -> 0 us
  other arithmetic: 17 us -> 0 us
  between operations: 14.6 us -> 0.74 us
  matrix products: 11.7 us -> 0 us
    pallas_call x0 -> x1, Pallas kernels: none -> 114 us  [body(): pl.pallas_call(functools.partial(kernel, sizes), out_shape=(jax.ShapeDtyp...]
    another operation x1 -> x0, loops' own time: 84.4 us -> none  [legendre_rows(): lax.scan(advance, (zeros, zeros), jnp.arange(ndeg, dtype=jnp.int32), unro...]
    all_to_all x7 -> x0, waiting for transfers between devices: 70.8 us -> none  [the longest x3 38.6 us: exchange_both(): parts = lax.all_to_all(parts, axis, split_axis=0, concat_axis=0, tiled=True)]
    all_to_all x7 -> x0, starting transfers between devices: 59 us -> none  [the longest x4 32.7 us: by_latitude(): lax.all_to_all(values, 'lat', split_axis=0, concat_axis=0, tiled=True)]
    all_to_all x1 -> x0, blocking collectives: 30.9 us -> none  [exchange_both(): parts = lax.all_to_all(parts, axis, split_axis=0, concat_axis=0, tiled=True)]
    another operation x19 -> x0, local copies, waits for them, and re-layouts: 17.4 us -> none
    dot_general x10 -> x0, matrix products: 11.7 us -> none  [the longest x2 3.12 us: analyse(): jnp.einsum('ibtcq,bxyrit->xrbcyq', spectrum, table, preferred_element_typ...]
    while x120 -> x0, other arithmetic: 10.1 us -> none
  transfers between devices with their start and end apart: 9 -> 0, of which waited for: 6 -> 0; matrix products, arithmetic and copies ran while one was open for 15% -> 0% of each run, Pallas kernels for 0% -> 0%
where the time goes in v1:
time: 119 us
  Pallas kernels  114 us (96%)
  local copies, waits for them, and re-layouts  4.12 us (3%)
    pallas_call x1, Pallas kernels, body(): pl.pallas_call(functools.partial(kernel, sizes), out_shape=(jax.ShapeDtyp...  114 us

profile of v1, /device:TPU:1, one launch (start us, length us, event | category | flops | bytes accessed | tf_op | source)
XLA Modules:
  0.0 119.2 jit_solution(2644541197987627358)
XLA Ops:
  0.6 0.0 copy-start.3
  0.6 0.0 copy-start.4
  0.7 1.2 reshape.27
  1.8 0.0 copy-start
  1.8 0.0 copy-start.1
  1.9 0.2 copy.12
  2.1 0.0 copy-start.2
  2.1 0.0 copy-start.5
  2.1 0.2 reshape.28.w_ref
  2.3 0.0 copy-done.3
  2.3 0.0 copy-done.4
  2.3 0.5 copy-done
  2.8 0.1 copy-done.1
  3.0 0.1 copy-done.2
  3.0 0.0 copy-done.5
  3.0 114.4 %block.1 = (bf16[512,384]{1,0:T(8,128)(2,1)S(1)}, bf16[64,1024]{1,0:T(8,128)(2,1)S(1)}) custom-call(bf16[512,384]{1,0:T(8,128)(2,1)S(1)} %bitcast.10, bf16[512,384]{1,0:T(8,128)(2,1)S(1)} %bitcast.11, bf16[64,1024]{1,0:T(8,128)(2,1)S(1)} %reshape.28.w_ref, bf16[128,384]{1,0:T(8,128)(2,1)S(1)} %copy-done.3, bf16[128,384]{1,0:T(8,128)(2,1)S(1)} %copy-done.2, ...), custom_call_target="tpu_custom_call" | custom-call | tf_op jit(solution)/shard_map/block/pallas_call | solution.py:384
  117.4 0.2 reshape.30
  117.6 0.8 reshape.31
  118.5 0.7 copy.14
  (1 shorter events, 0.0 us)
Async XLA Ops:
  0.6 1.7 %copy-start.3 = (bf16[128,384]{1,0:T(8,128)(2,1)S(1)}, bf16[128,384]{1,0:T(8,128)(2,1)}, u32[]{:S(2)}) copy-start(bf16[128,384]{1,0:T(8,128)(2,1)} %constant.8.clone.forward_ref) | copy-start | bytes 294916
  0.6 1.7 %copy-start.4 = (f32[128,128]{1,0:T(8,128)S(1)}, f32[128,128]{1,0:T(8,128)}, u32[]{:S(2)}) copy-start(f32[128,128]{1,0:T(8,128)} %constant.10.clone.seeds_ref) | copy-start | bytes 196612
  1.8 1.0 copy-start
  1.8 1.1 copy-start.1
  2.1 1.0 copy-start.2
  2.1 0.9 copy-start.5

commit v2 on v1

v2 whole, which is shorter than its diff:
```python
import functools
import math

import jax
import jax.numpy as jnp
import numpy as np
from jax import lax
from jax.experimental import pallas as pl
from jax.experimental.pallas import tpu as pltpu
from jax.sharding import PartitionSpec as P

MESH = pl.DeviceIdType.MESH
BF16 = jnp.bfloat16
F32 = jnp.float32
M_DEV = 4
ROWS = 8
SLAB = 64
CHUNKS = 2
MC = M_DEV // CHUNKS
SEM_COEFF, SEM_GRADS, SEM_RESULT, SEM_RING = (8 * CHUNKS + i for i in range(4))


def fourier_tables(nlon, norders):
    cols = np.arange(nlon, dtype=np.int32)[None, :]
    rows = np.arange(norders, dtype=np.int32)[:, None]
    phase = (cols * rows % nlon).astype(np.float32) * np.float32(2.0 * math.pi / nlon)
    cosine, sine = np.cos(phase), np.sin(phase)
    doubled = np.where(rows == 0, 1.0, 2.0).astype(np.float32)
    forward = np.stack([cosine / np.float32(nlon), -sine / np.float32(nlon)])
    inverse = np.stack([doubled * cosine, -doubled * sine])

    def by_chunk(table):
        table = table.reshape(2, norders // M_DEV, CHUNKS, MC, nlon).transpose(2, 0, 1, 3, 4)
        return jnp.asarray(table.reshape(2 * norders, nlon), BF16)

    return by_chunk(forward), by_chunk(inverse)


def legendre_seeds(nlat, norders):
    theta = np.float32(math.pi) * (np.arange(nlat, dtype=np.float32) + np.float32(0.5)) / np.float32(nlat)
    theta = theta.astype(np.float64)
    seeds = np.zeros((norders // M_DEV, 8, nlat), np.float32)
    for m in range(norders):
        scale = math.lgamma(2.0 * m + 2.0) - m * math.log(4.0) - 2.0 * math.lgamma(m + 1.0)
        start = 0.5 * math.log(0.5) + 0.5 * scale + m * np.log(np.sin(theta))
        seeds[m // M_DEV, m % M_DEV] = np.exp(start).astype(np.float32)
    rows = np.zeros((8, nlat), np.float32)
    rows[0] = np.cos(theta)
    rows[1] = math.pi * np.sin(theta) / nlat
    return jnp.asarray(seeds.reshape(-1, nlat)), jnp.asarray(rows)


def swap_halves(tile):
    return pltpu.roll(tile, 64, axis=1)


def low_lanes(shape):
    return lax.broadcasted_iota(jnp.int32, shape, 1) < 64


def gelu_slope(values):
    return 0.5 * (1.0 + lax.erf(values * (1.0 / math.sqrt(2.0)))) + values * jnp.exp(
        -0.5 * values * values
    ) * (1.0 / math.sqrt(2.0 * math.pi))


def kernel(
    sizes,
    x_hbm,
    g_hbm,
    w_hbm,
    forward_hbm,
    inverse_hbm,
    seeds_hbm,
    rows_hbm,
    out_ref,
    gw_ref,
    by_lat_out,
    by_lat_in,
    by_deg_out,
    by_deg_in,
    wide,
    coeff_all,
    grads_all,
    mixing,
    coeff_t,
    result_out,
    result_in,
    combined,
    fgrad,
    stage,
    leg,
    analysis,
    analysis_t,
    synthesis,
    synthesis_t,
    x_ref,
    g_ref,
    w_ref,
    forward_ref,
    inverse_ref,
    seeds_ref,
    rows_ref,
    send_sem,
    recv_sem,
    load_sem,
):
    loads = [
        pltpu.make_async_copy(src, dst, load_sem.at[i])
        for i, (src, dst) in enumerate(
            (
                (x_hbm, x_ref),
                (forward_hbm, forward_ref),
                (w_hbm, w_ref),
                (seeds_hbm, seeds_ref),
                (rows_hbm, rows_ref),
                (inverse_hbm, inverse_ref),
                (g_hbm, g_ref),
            )
        )
    ]
    for load in loads:
        load.start()
    n_dp, n_lat, n_lon = sizes
    n_x = min(n_lon, 4)
    n_zlo = n_lat // 2
    n_z = n_zlo * (n_lon // n_x)
    orders = n_lat * M_DEV
    part_orders = orders // CHUNKS
    n_deg = n_lat * n_lon
    nlat = n_lat * ROWS
    hops = n_dp // 2
    s = lax.axis_index("dp")
    a = lax.axis_index("lat")
    y = lax.axis_index("lon")
    chip, core = lax.div(a, 2), lax.rem(a, 2)
    x, zhi = lax.rem(y, n_x), lax.div(y, n_x)
    z = zhi * n_zlo + chip

    def over_degree_group(visit):
        def step(k, carry):
            half = lax.div(k + 1, 2)
            off = jnp.where(lax.rem(k, 2) == 1, n_z // 2 - half, n_z // 2 + half)
            zt = lax.rem(z + off, n_z)
            zl, zh = lax.rem(zt, n_zlo), lax.div(zt, n_zlo)
            for dx in list(range(n_x // 2, 0, -1)) + list(range(n_x // 2 + 1, n_x)) + [0]:
                for dc in (1, 0):
                    la = zl * 2 + lax.rem(core + dc, 2)
                    lo = zh * n_x + lax.rem(x + dx, n_x)
                    if dx == 0 and dc == 0:
                        pl.when(k < n_z - 1)(functools.partial(visit, la, lo))
                    else:
                        visit(la, lo)
            return carry

        lax.fori_loop(0, n_z, step, 0)

    def over_lat_group(visit):
        for d in range(n_zlo - 1, 0, -1):
            for q in (chip + d, chip - d):

                @pl.when((q >= 0) & (q < n_zlo))
                def _(q=q):
                    visit(q * 2)
                    visit(q * 2 + 1)

        visit(chip * 2 + 1 - core)

    def over_dp_group(visit):
        for d in list(range(n_dp // 2, 0, -1)) + list(range(n_dp // 2 + 1, n_dp)):
            visit(lax.rem(s + d, n_dp))

    def remote(src, dst, sem, device):
        pltpu.make_async_remote_copy(
            src_ref=src,
            dst_ref=dst,
            send_sem=send_sem.at[sem],
            recv_sem=recv_sem.at[sem],
            device_id=device,
            device_id_type=MESH,
        ).start()

    def local(src, dst, sem):
        pltpu.make_async_copy(src, dst, recv_sem.at[sem]).start()

    def arrived(ref, sem):
        pltpu.make_async_copy(ref, ref, recv_sem.at[sem]).wait()

    def sent(ref, sem):
        pltpu.make_async_copy(ref, ref, send_sem.at[sem]).wait()

    def send_by_lat(e, k, h):
        src, dst, sem = by_lat_out.at[k, h], by_lat_in.at[k, h], e * CHUNKS + h
        over_lat_group(lambda j: remote(src.at[j], dst.at[a], sem, {"lat": j}))
        local(src.at[a], dst.at[a], sem)

    def send_to_degrees(e, k, h):
        src, dst, sem = by_deg_out.at[k, h], by_deg_in.at[k, h], e * CHUNKS + h
        mine = y * n_lat + a
        over_degree_group(
            lambda la, lo: remote(src.at[la * n_lon + lo], dst.at[mine], sem, {"lat": la, "lon": lo})
        )
        local(src.at[a * n_lon + y], dst.at[mine], sem)

    def send_to_orders(e, k, h):
        src, dst, sem = by_deg_out.at[k, h], by_deg_in.at[k, h], e * CHUNKS + h
        mine = a * n_lon + y
        over_degree_group(
            lambda la, lo: remote(src.at[lo * n_lat + la], dst.at[mine], sem, {"lat": la, "lon": lo})
        )
        local(src.at[y * n_lat + a], dst.at[mine], sem)

    def by_lat_arrived(e, k, h):
        arrived(by_lat_in.at[k, h], e * CHUNKS + h)

    def by_deg_arrived(e, k, h):
        arrived(by_deg_in.at[k, h], e * CHUNKS + h)

    def to_spectrum(table_ref, values_ref, k, h):
        out = lax.dot_general(
            table_ref[h * 2 * part_orders : (h + 1) * 2 * part_orders, :],
            values_ref[...],
            (((1,), (1,)), ((), ())),
            preferred_element_type=F32,
        )
        low = low_lanes((part_orders, 128))
        for j in range(ROWS // 2):
            real = out[:part_orders, j * 128 : (j + 1) * 128]
            imag = out[part_orders:, j * 128 : (j + 1) * 128]
            stage[pl.ds(2 * j, part_orders, stride=ROWS), :] = jnp.where(low, real, swap_halves(imag))
            stage[pl.ds(2 * j + 1, part_orders, stride=ROWS), :] = jnp.where(
                low, swap_halves(real), imag
            )
        by_lat_out[k, h] = (
            stage[: part_orders * ROWS, :].astype(BF16).reshape(n_lat, MC * ROWS, 128)
        )

    def to_degrees(tables, k, h):
        for m in range(MC):
            part = by_lat_in[k, h, :, m * ROWS : (m + 1) * ROWS, :]
            part = part.astype(F32).reshape(nlat, 128).astype(BF16)
            stage[pl.ds(m, n_deg, stride=MC), :] = jnp.dot(
                tables[h * MC + m], part, preferred_element_type=F32
            )
        return stage[: n_deg * MC, :].reshape(n_deg, MC, 128).astype(BF16)

    def gather_wide(k, h):
        for j in range(n_lon):
            part = by_deg_in[k, h, j * n_lat : (j + 1) * n_lat]
            wide[h, :, j * 128 : (j + 1) * 128] = (
                part.astype(F32).reshape(part_orders, 128).astype(BF16)
            )

    def scatter_wide(value, k, h):
        for j in range(n_lon):
            part = value[:, j * 128 : (j + 1) * 128].reshape(n_lat, MC, 128)
            by_deg_out[k, h, j * n_lat : (j + 1) * n_lat] = part.astype(BF16)

    def to_rows(tables, k_in, k, h):
        stage[: n_deg * MC, :] = by_deg_in[k_in, h].astype(F32).reshape(n_deg * MC, 128)
        parts = []
        for m in range(MC):
            part = stage[pl.ds(m, n_deg, stride=MC), :].astype(BF16)
            out = jnp.dot(tables[h * MC + m], part, preferred_element_type=F32)
            parts.append(out.reshape(n_lat, ROWS, 128))
        both = jnp.stack(parts, axis=1).reshape(n_lat, MC * ROWS, 128)
        by_lat_out[k, h] = both.astype(BF16)

    def combine(k, h):
        stage[: part_orders * ROWS, :] = by_lat_in[k, h].astype(F32).reshape(part_orders * ROWS, 128)
        low = low_lanes((part_orders, 128))
        for j in range(ROWS // 2):
            even = stage[pl.ds(2 * j, part_orders, stride=ROWS), :]
            odd = stage[pl.ds(2 * j + 1, part_orders, stride=ROWS), :]
            real = jnp.where(low, even, swap_halves(odd))
            imag = jnp.where(low, swap_halves(even), odd)
            combined[
                h * 2 * part_orders : (h + 1) * 2 * part_orders, j * 128 : (j + 1) * 128
            ] = jnp.concatenate([real, imag], axis=0).astype(BF16)

    def to_grid(table_ref, use):
        for j in range(ROWS // 2):
            rows = slice(j * 128, (j + 1) * 128)
            use(
                rows,
                lax.dot_general(
                    combined[:, rows],
                    table_ref[...],
                    (((0,), (0,)), ((), ())),
                    preferred_element_type=F32,
                ),
            )

    barrier = pltpu.get_barrier_semaphore()

    def greet(device):
        pl.semaphore_signal(barrier, inc=1, device_id=device, device_id_type=MESH)

    over_degree_group(lambda la, lo: greet({"lat": la, "lon": lo}))
    over_dp_group(lambda j: greet({"dp": j}))

    low = low_lanes((64, 128))

    def upper(block, start=0, size=64):
        return pl.ds(pl.multiple_of(block * 128 + start, 32), size)

    def fill_lower(block):
        rows = pl.ds(pl.multiple_of(block * 128 + 64, 64), 64)
        for i in range(n_lon):
            tile = slice(i * 128, (i + 1) * 128)
            turned = swap_halves(mixing[upper(block), tile].astype(F32))
            mixing[rows, tile] = jnp.where(low, -turned, turned).astype(BF16)

    right, left = lax.rem(s + 1, n_dp), lax.rem(s + n_dp - 1, n_dp)

    def from_left(k):
        return lax.rem(s + n_dp - k, n_dp)

    def from_right(k):
        return lax.rem(s + k, n_dp)

    def halves(k):
        return [
            (half, to_right, SEM_RING + (k * 2 + half) * 2 + to_right)
            for half in (0, 1)
            for to_right in (0, 1)
            if k < hops - 1 or half == to_right
        ]

    def pass_weights(k, half=None):
        for part, to_right, sem in halves(k):
            if half is None or part == half:
                block = from_left(k) if to_right else from_right(k)
                rows = mixing.at[upper(block, 32 * part, 32), :]
                remote(rows, rows, sem, {"dp": right if to_right else left})

    def weights_arrived(k, half):
        for part, _, sem in halves(k):
            if part == half:
                arrived(mixing.at[pl.ds(0, 32), :], sem)
        if k < hops - 1:
            pass_weights(k + 1, half)
        if half == 1:
            fill_lower(from_right(k + 1))
            if k < hops - 1:
                fill_lower(from_left(k + 1))

    loads[0].wait()
    loads[1].wait()
    for h in range(CHUNKS):
        to_spectrum(forward_ref, x_ref, 0, h)
    pl.semaphore_wait(barrier, n_deg - 1 + n_dp - 1)

    for h in range(CHUNKS):
        send_by_lat(0, 0, h)
    loads[2].wait()
    weights = w_ref[...].astype(F32)
    for i in range(n_lon // 2):
        real = weights[:, 0, i * 128 : (i + 1) * 128]
        imag = weights[:, 1, i * 128 : (i + 1) * 128]
        mixing[upper(s), 2 * i * 128 : (2 * i + 1) * 128] = jnp.where(
            low, real, swap_halves(imag)
        ).astype(BF16)
        mixing[upper(s), (2 * i + 1) * 128 : (2 * i + 2) * 128] = jnp.where(
            low, swap_halves(real), imag
        ).astype(BF16)
    pass_weights(0)
    fill_lower(s)

    for load in loads[3:]:
        load.wait()

    order = (a * M_DEV + lax.broadcasted_iota(jnp.int32, (8, nlat), 0)).astype(F32)
    order_sq = order * order
    cosine = jnp.broadcast_to(rows_ref[0:1, :], (8, nlat))
    start = seeds_ref[pl.ds(pl.multiple_of(a * 8, 8), 8), :]

    def advance(degree, carry):
        older, newer, deg = carry
        below = deg - 1.0
        scale_a = jnp.sqrt(
            jnp.maximum(4.0 * deg * deg - 1.0, 0.0) / jnp.maximum(deg * deg - order_sq, 1.0)
        )
        scale_b = jnp.sqrt(
            jnp.maximum(below * below - order_sq, 0.0)
            / jnp.maximum(4.0 * (below * below) - 1.0, 1.0)
        )
        general = scale_a * (cosine * newer - scale_b * older)
        value = jnp.where(deg < order, 0.0, jnp.where(deg == order, start, general))
        leg[pl.ds(pl.multiple_of(degree * 8, 8), 8), :] = value
        return newer, value, deg + 1.0

    zeros = start * 0.0
    lax.fori_loop(0, n_deg, advance, (zeros, zeros, zeros), unroll=8)
    for m in range(M_DEV):
        table = leg[pl.ds(m, n_deg, stride=8), :]
        weighted = table * rows_ref[1:2, :]
        synthesis[m] = table.astype(BF16)
        analysis[m] = weighted.astype(BF16)
        synthesis_t[m] = table.T.astype(BF16)
        analysis_t[m] = weighted.T.astype(BF16)

    for half in (0, 1):
        weights_arrived(0, half)
    for h in range(CHUNKS):
        by_lat_arrived(0, 0, h)
        by_deg_out[0, h] = to_degrees(analysis, 0, h)
        send_to_degrees(1, 0, h)
        if h == 0 and hops > 1:
            for half in (0, 1):
                weights_arrived(1, half)
    for k in range(2, hops):
        for half in (0, 1):
            weights_arrived(k, half)

    for h in range(CHUNKS):
        by_deg_arrived(1, 0, h)
        gather_wide(0, h)
        scatter_wide(jnp.dot(wide[h], mixing[...], preferred_element_type=F32), 1, h)
        send_to_orders(2, 1, h)

    for h in range(CHUNKS):
        coeff = by_deg_in.at[0, h]
        over_dp_group(lambda j: remote(coeff, coeff_all.at[s, h], SEM_COEFF, {"dp": j}))
        local(coeff, coeff_all.at[s, h], SEM_COEFF)

    for h in range(CHUNKS):
        by_deg_arrived(2, 1, h)
        to_rows(synthesis_t, 1, 1, h)
        send_by_lat(3, 1, h)
    for h in range(CHUNKS):
        by_lat_arrived(3, 1, h)
        combine(1, h)

    def slope(rows, filtered):
        fgrad[rows, :] = (g_ref[rows, :].astype(F32) * gelu_slope(filtered)).astype(BF16)

    to_grid(inverse_ref, slope)
    for h in range(CHUNKS):
        to_spectrum(inverse_ref, fgrad, 2, h)
        send_by_lat(4, 2, h)
    for h in range(CHUNKS):
        by_lat_arrived(4, 2, h)
        by_deg_out[2, h] = to_degrees(synthesis, 2, h)
        send_to_degrees(5, 2, h)

    arrived(coeff_all, SEM_COEFF)
    for j in range(n_lon):
        part = coeff_all[:, :, j * n_lat : (j + 1) * n_lat].astype(F32).reshape(n_dp * orders, 128)
        coeff_t[j * 128 : (j + 1) * 128, :] = part.T.astype(BF16)

    for h in range(CHUNKS):
        by_deg_arrived(5, 2, h)
        gather_wide(2, h)
        scatter_wide(
            lax.dot_general(
                wide[h], mixing[...], (((1,), (1,)), ((), ())), preferred_element_type=F32
            ),
            3,
            h,
        )
        send_to_orders(6, 3, h)

        def grads_block(j, h=h):
            return by_deg_in.at[2, h, pl.ds(j * n_lat, n_lat)]

        over_dp_group(lambda j: remote(grads_block(j), grads_all.at[s, h], SEM_GRADS, {"dp": j}))
        local(grads_block(s), grads_all.at[s, h], SEM_GRADS)

    for h in range(CHUNKS):
        by_deg_arrived(6, 3, h)
        to_rows(analysis_t, 3, 3, h)
        send_by_lat(7, 3, h)

    arrived(grads_all, SEM_GRADS)
    total = jnp.dot(
        coeff_t[...],
        grads_all[...].astype(F32).reshape(n_dp * orders, 128).astype(BF16),
        preferred_element_type=F32,
    )
    for j in range(n_lon):
        real = total[j * 128 : j * 128 + 64]
        imag = swap_halves(total[j * 128 + 64 : (j + 1) * 128])
        result_out[j] = (jnp.where(low, real + imag, real - imag) * (1.0 / n_dp)).astype(BF16)
    over_dp_group(lambda j: remote(result_out.at[j], result_in.at[s], SEM_RESULT, {"dp": j}))
    local(result_out.at[s], result_in.at[s], SEM_RESULT)

    for h in range(CHUNKS):
        by_lat_arrived(7, 3, h)
        combine(3, h)

    def finish(rows, branch):
        out_ref[rows, :] = branch

    to_grid(forward_ref, finish)

    arrived(result_in, SEM_RESULT)
    for i in range(n_lon // 2):
        even, odd = result_in[2 * i].astype(F32), result_in[2 * i + 1].astype(F32)
        both = jnp.stack(
            [jnp.where(low, even, swap_halves(odd)), jnp.where(low, swap_halves(even), odd)], axis=1
        )
        gw_ref[:, :, i * 128 : (i + 1) * 128] = both.astype(BF16)

    for h in range(CHUNKS):
        for e, k in ((0, 0), (3, 1), (4, 2), (7, 3)):
            sent(by_lat_out.at[k, h, pl.ds(0, n_lat - 1)], e * CHUNKS + h)
        for e, k in ((1, 0), (2, 1), (5, 2), (6, 3)):
            sent(by_deg_out.at[k, h, pl.ds(0, n_deg - 1)], e * CHUNKS + h)
    sent(coeff_all.at[pl.ds(0, n_dp - 1)], SEM_COEFF)
    sent(grads_all.at[pl.ds(0, n_dp - 1)], SEM_GRADS)
    sent(result_in.at[pl.ds(0, n_dp - 1)], SEM_RESULT)
    for k in range(hops):
        for _, _, sem in halves(k):
            sent(mixing.at[pl.ds(0, 32), :], sem)


def body(sizes, field, cotangent, spectral_weight):
    n_dp, n_lat, n_lon = sizes
    nlon = field.shape[3]
    orders, n_deg, nlat = n_lat * M_DEV, n_lat * n_lon, n_lat * ROWS
    width = n_lon * 128
    rows = ROWS * SLAB
    forward, inverse = fourier_tables(nlon, orders)
    seeds, lat_rows = legendre_seeds(nlat, orders)
    vmem = pl.BlockSpec(memory_space=pltpu.VMEM)
    hbm = pl.BlockSpec(memory_space=pltpu.HBM)
    operands = (
        field.reshape(rows, nlon),
        cotangent.reshape(rows, nlon),
        spectral_weight.reshape(64, 2, n_lon * SLAB),
        forward,
        inverse,
        seeds,
        lat_rows,
    )
    n_sem = 8 * CHUNKS + 3 + 2 * n_dp
    branch, grad_weight = pl.pallas_call(
        functools.partial(kernel, sizes),
        out_shape=(
            jax.ShapeDtypeStruct((rows, nlon), F32),
            jax.ShapeDtypeStruct((64, 2, n_lon * SLAB), BF16),
        ),
        in_specs=[hbm] * 7,
        out_specs=(vmem, vmem),
        scratch_shapes=[
            pltpu.VMEM((4, CHUNKS, n_lat, MC * ROWS, 128), BF16),
            pltpu.VMEM((4, CHUNKS, n_lat, MC * ROWS, 128), BF16),
            pltpu.VMEM((4, CHUNKS, n_deg, MC, 128), BF16),
            pltpu.VMEM((4, CHUNKS, n_deg, MC, 128), BF16),
            pltpu.VMEM((CHUNKS, orders // CHUNKS, width), BF16),
            pltpu.VMEM((n_dp, CHUNKS, n_deg, MC, 128), BF16),
            pltpu.VMEM((n_dp, CHUNKS, n_lat, MC, 128), BF16),
            pltpu.VMEM((width, width), BF16),
            pltpu.VMEM((width, n_dp * orders), BF16),
            pltpu.VMEM((n_dp, 64, 128), BF16),
            pltpu.VMEM((n_dp, 64, 128), BF16),
            pltpu.VMEM((2 * orders, rows), BF16),
            pltpu.VMEM((rows, nlon), BF16),
            pltpu.VMEM((max(n_deg * MC, orders * ROWS // CHUNKS), 128), F32),
            pltpu.VMEM((n_deg * 8, nlat), F32),
            pltpu.VMEM((M_DEV, n_deg, nlat), BF16),
            pltpu.VMEM((M_DEV, nlat, n_deg), BF16),
            pltpu.VMEM((M_DEV, n_deg, nlat), BF16),
            pltpu.VMEM((M_DEV, nlat, n_deg), BF16),
            *(pltpu.VMEM(operand.shape, operand.dtype) for operand in operands),
            pltpu.SemaphoreType.DMA((n_sem,)),
            pltpu.SemaphoreType.DMA((n_sem,)),
            pltpu.SemaphoreType.DMA((len(operands),)),
        ],
        compiler_params=pltpu.CompilerParams(
            collective_id=0, has_side_effects=True, vmem_limit_bytes=60 * 1024 * 1024
        ),
        name="block",
    )(*operands)
    return (
        (cotangent.astype(F32) + branch.reshape(cotangent.shape)).astype(BF16),
        grad_weight.reshape(64, 1, 2, n_lon * SLAB),
    )


def solution(mesh):
    sizes = (mesh.shape["dp"], mesh.shape["lat"], mesh.shape["lon"])
    return jax.shard_map(
        functools.partial(body, sizes),
        mesh=mesh,
        in_specs=(
            P("dp", "lat", "lon", None),
            P("dp", "lat", "lon", None),
            P("dp", ("lat", "lon"), None, None),
        ),
        out_specs=(P("dp", "lat", "lon", None), P("dp", ("lat", "lon"), None, None)),
        check_vma=False,
    )
```

time: 119 us -> 102 us (0.86)
  Pallas kernels: 114 us -> 98.3 us
  local copies, waits for them, and re-layouts: 4.12 us -> 0.66 us
  other arithmetic: 0 us -> 2 us
    pallas_call x1, Pallas kernels: 114 us -> 98.3 us  [body(): pl.pallas_call(functools.partial(kernel, sizes), out_shape=(jax.ShapeDtyp...]
    reshape x5 -> x0, local copies, waits for them, and re-layouts: 2.6 us -> none  [the longest x3 1.58 us: body(): spectral_weight.reshape(64, 2, n_lon, 64).transpose(0, 2, 1, 3)]
    convert_element_type x0 -> x1, other arithmetic: none -> 2 us  [body(): (cotangent.astype(F32) + branch.reshape(cotangent.shape)).astype(BF16)]
where the time goes in v2:
time: 102 us
  Pallas kernels  98.3 us (96%)
  other arithmetic  2 us (2%)
    pallas_call x1, Pallas kernels, body(): pl.pallas_call(functools.partial(kernel, sizes), out_shape=(jax.ShapeDtyp...  98.3 us

profile of v2, /device:TPU:1, one launch (start us, length us, event | category | flops | bytes accessed | tf_op | source)
XLA Modules:
  0.0 101.7 jit_solution(17783284810209774488)
XLA Ops:
  0.6 0.0 copy-start
  0.6 98.3 %block.1 = (f32[512,384]{1,0:T(8,128)}, bf16[64,2,512]{2,1,0:T(2,128)(2,1)}) custom-call(bf16[512,384]{1,0:T(8,128)(2,1)} %bitcast.9, bf16[512,384]{1,0:T(8,128)(2,1)} %bitcast.7, bf16[64,2,512]{2,1,0:T(2,128)(2,1)} %bitcast.10, bf16[128,384]{1,0:T(8,128)(2,1)} %constant.8.clone.forward_hbm, bf16[128,384]{1,0:T(8,128)(2,1)} %constant.9.clone.inverse_hbm, ...), custom_call_target="tpu_custom_call" | custom-call | tf_op jit(solution)/shard_map/block/pallas_call | solution.py:538
  99.0 0.0 copy-done
  99.0 0.0 copy-start.1
  99.0 2.0 %add_convert_fusion = bf16[1,8,64,384]{3,2,1,0:T(8,128)(2,1)} fusion(f32[1,8,64,384]{3,2,1,0:T(8,128)} %bitcast.8, bf16[1,8,64,384]{3,2,1,0:T(8,128)(2,1)S(1)} %copy-done), kind=kLoop, calls=%fused_computation | loop fusion | flops 589824 | bytes 1572864 | tf_op jit(solution)/shard_map/convert_element_type | solution.py:577
  101.0 0.0 copy-done.1
  101.0 0.7 copy.11
Async XLA Ops:
  0.6 98.4 %copy-start = (bf16[1,8,64,384]{3,2,1,0:T(8,128)(2,1)S(1)}, bf16[1,8,64,384]{3,2,1,0:T(8,128)(2,1)}, u32[]{:S(2)}) copy-start(bf16[1,8,64,384]{3,2,1,0:T(8,128)(2,1)} %param.8) | copy-start | bytes 1179652
  99.0 2.0 %copy-start.1 = (bf16[64,2,512]{2,1,0:T(2,128)(2,1)S(1)}, bf16[64,2,512]{2,1,0:T(2,128)(2,1)}, u32[]{:S(2)}) copy-start(bf16[64,2,512]{2,1,0:T(2,128)(2,1)} %get-tuple-element.5) | copy-start | bytes 393220
